TPU v7x, 256 devices: a whole 4x4x8 slice. The times are simulated.
256 devices in a mesh: bl: 32 (over x, z), ta: 8 (over y, core).
Axes of the slice: x: 4, y: 4, z: 8, core: 2. Of those that a mesh axis runs over, the one named last changes fastest.
Arguments:
- log_amplitude: bfloat16 [8192, 8, 1536], P('bl', 'ta'), may hold values from -2.5 to 2.5
- phase: bfloat16 [8192, 8, 1536], P('bl', 'ta'), may hold values from -4 to 4
- redundant_group_index: int32 [8192], P('bl'), may hold values from 0 to 223, as said below
- antenna_couples: int32 [8192, 2], P('bl'), may hold values from 0 to 349, as said below
- tile_flag_mask: int32 [8192, 12], P(('bl', 'ta')), may hold values from 0 to 1, as said below
- inverse: float32 [2, 350, 350], replicated, may hold values from -1 to 1
- integration_kernel: float32 [8, 8], replicated, may hold values from 0.01 to 1
- channel_kernel: bfloat16 [7, 128, 128], replicated, may hold values from 0.0009994507 to 1
Outputs:
- antenna_gains: float32 [2, 350, 8, 1536], P(None, None, 'ta')
- filled: float32 [2, 8192, 8, 1536], P(None, ('bl', 'ta'))
Inputs may be any that keep to these rules, and one draw needn't show every extreme that they name: `redundant_group_index`: every group from 0 to 223 holds at least one baseline. `antenna_couples`: the two antennas of a baseline differ. `tile_flag_mask`: both neighbouring tiles of a flagged tile are unflagged.
All inputs are finite; a program needn't handle non-finite values.
Results may differ from a plain program's by a relative error of at most 0.0029.
Values may be sent and summed in bfloat16 or wider, within the bound.
A program may use at most 64 MiB of HBM per device.

v0:
```python
import jax
import jax.numpy as jnp
from jax import lax
from jax.sharding import PartitionSpec as P

ANTENNA_COUNT = 350
NGRP = 224


def mix_channels(values, channel_kernel):
    span_tiles = (channel_kernel.shape[0] - 1) // 2
    tile_width = channel_kernel.shape[1]
    leading = values.shape[:-1]
    tile_count = values.shape[-1] // tile_width
    tiled = values.reshape(leading + (tile_count, tile_width))
    pad_spec = [(0, 0)] * len(leading) + [(span_tiles, span_tiles), (0, 0)]
    padded = jnp.pad(tiled, pad_spec)
    summed = jnp.zeros(leading + (tile_count, tile_width), jnp.float32)
    for offset in range(2 * span_tiles + 1):
        window = lax.slice_in_dim(padded, offset, offset + tile_count, axis=len(leading))
        summed = summed + jnp.einsum(
            "...kj,ij->...ki", window, channel_kernel[offset], preferred_element_type=jnp.float32
        )
    return summed.reshape(leading + (tile_count * tile_width,))


def fill_block(calibrated, tile_flag_mask, integration_kernel, channel_kernel):
    tile_width = channel_kernel.shape[1]
    weight = jnp.repeat((1 - tile_flag_mask).astype(jnp.bfloat16), tile_width, axis=1)
    masked = calibrated * weight[None, :, None, :]
    mixed = mix_channels(masked, channel_kernel)
    numerator = jnp.einsum(
        "tu,kbuf->kbtf", integration_kernel, mixed, precision=lax.Precision.HIGHEST
    )
    weight_mix = mix_channels(weight, channel_kernel)
    denominator = jnp.sum(integration_kernel, axis=1)[None, :, None] * weight_mix[:, None, :]
    keep = weight.astype(jnp.float32)[None, :, None, :]
    return keep * calibrated.astype(jnp.float32) + (1.0 - keep) * numerator / denominator[None]


def solve_columns(inverse, normal_right_side):
    return jnp.einsum("sab,sbtf->satf", inverse, normal_right_side, precision=lax.Precision.HIGHEST)


def on_device(
    log_amplitude,
    phase,
    redundant_group_index,
    antenna_couples,
    tile_flag_mask,
    inverse,
    integration_kernel,
    channel_kernel,
):
    stacked_terms = jnp.stack([log_amplitude, phase])
    first_antenna = antenna_couples[:, 0]
    second_antenna = antenna_couples[:, 1]
    group_hot = (
        redundant_group_index[:, None] == jnp.arange(NGRP, dtype=jnp.int32)[None, :]
    ).astype(jnp.bfloat16)
    antenna_labels = jnp.arange(ANTENNA_COUNT, dtype=jnp.int32)[None, :]
    first_onehot = (first_antenna[:, None] == antenna_labels).astype(jnp.float32)
    second_onehot = (second_antenna[:, None] == antenna_labels).astype(jnp.float32)
    signed_float = jnp.stack([first_onehot + second_onehot, first_onehot - second_onehot])
    group_part = jnp.einsum(
        "bg,sbtf->sgtf", group_hot, stacked_terms, preferred_element_type=jnp.float32
    )
    count_part = jnp.sum(group_hot.astype(jnp.float32), axis=0)
    group_sums, group_counts = lax.psum((group_part, count_part), "bl")
    group_mean = group_sums / group_counts[None, :, None, None]
    fit_residual = stacked_terms.astype(jnp.float32) - jnp.take(
        group_mean, redundant_group_index, axis=1
    )
    rhs_part = jnp.einsum(
        "sba,sbtf->satf", signed_float, fit_residual, precision=lax.Precision.HIGHEST
    )
    normal_right_side = lax.psum(rhs_part, "bl")
    antenna_gains = solve_columns(inverse, normal_right_side)
    amplitude_gain = antenna_gains[0]
    phase_gain_term = antenna_gains[1]
    calibrated_amplitude = (
        log_amplitude.astype(jnp.float32)
        - jnp.take(amplitude_gain, first_antenna, axis=0)
        - jnp.take(amplitude_gain, second_antenna, axis=0)
    )
    calibrated_phase = (
        phase.astype(jnp.float32)
        - jnp.take(phase_gain_term, first_antenna, axis=0)
        + jnp.take(phase_gain_term, second_antenna, axis=0)
    )
    magnitude = jnp.exp(calibrated_amplitude)
    calibrated = jnp.stack(
        [magnitude * jnp.cos(calibrated_phase), magnitude * jnp.sin(calibrated_phase)]
    ).astype(jnp.bfloat16)
    filled = fill_block(
        lax.all_to_all(calibrated, "ta", split_axis=1, concat_axis=2, tiled=True),
        tile_flag_mask,
        integration_kernel,
        channel_kernel,
    )
    return (antenna_gains, filled)


def solution(mesh):
    in_specs = (
        P("bl", "ta", None),
        P("bl", "ta", None),
        P("bl"),
        P("bl", None),
        P(("bl", "ta"), None),
        P(),
        P(),
        P(),
    )
    out_specs = (P(None, None, "ta", None), P(None, ("bl", "ta"), None, None))
    return jax.shard_map(
        on_device, mesh=mesh, in_specs=in_specs, out_specs=out_specs, check_vma=False
    )
```

profile of v0, /device:TPU:1, one launch (start us, length us, event | category | flops | bytes accessed | tf_op | source)
XLA Modules:
  0.0 452.8 jit_solution(7222060183240848524)
XLA Ops:
  7.2 0.0 copy-start
  7.2 0.0 all-reduce.5.cloned.1.call-start
  7.2 3.5 convolution_bitcast_fusion
  10.7 0.0 copy-start.10
  10.7 0.0 copy-start.12
  10.8 0.0 all-reduce.5.cloned.1.call-update
  10.8 0.0 all-reduce.7.cloned.1.call-start
  10.8 0.6 copy-done.10
  11.4 0.1 convert_reduce_fusion
  11.5 64.8 %psum.22 = f32[224]{0:T(256)S(1)} all-reduce(f32[224]{0:T(256)S(1)} %convert_reduce_fusion), channel_id=1, replica_groups=mesh['bl'=32,'ta'=8] {'bl'}, use_global_device_ids=true, to_apply=%region_2.0 | all-reduce | flops 224 | bytes 1792 | tf_op jit(solution)/shard_map/psum | solution.py:69
  76.3 0.0 copy-done.12
  76.4 0.1 convert_add_fusion
  76.4 92.5 %all-reduce.5.cloned.1.call-done = f32[2,224,1,1536]{3,1,0,2:T(8,128)} async-done(((f32[2,224,1,1536]{3,1,0,2:T(8,128)}), f32[2,224,1,1536]{3,1,0,2:T(8,128)}) %all-reduce.5.cloned.1.call-update) | async-done | bytes 2752528 | tf_op jit(solution)/shard_map/psum | solution.py:69
  169.0 2.1 divide_bitcast_fusion
  171.0 3.7 copy.54
  174.7 0.0 copy-start.4
  174.7 0.0 copy-start.6
  174.7 7.3 %gather_fusion = f32[256,2,1536]{2,1,0:T(2,128)} fusion(f32[2,224,1536]{2,0,1:T(2,128)} %copy.54, s32[1024]{0:T(1024)S(1)} %pad_clamp_fusion.2), kind=kCustom, calls=%fused_computation.4 | custom fusion | bytes 6292480 | tf_op jit(solution)/shard_map/jit(_take)/gather | solution.py:71
  182.0 0.0 copy-done.4
  182.0 0.0 copy-done.6
  182.0 8.8 %fusion.3 = f32[2,350,1536]{2,1,0:T(8,128)} fusion(f32[256,2,1536]{2,1,0:T(2,128)} %gather_fusion, bf16[1,256,1536]{2,1,0:T(8,128)(2,1)S(1)} %bitcast.201, bf16[1,256,1536]{2,1,0:T(8,128)(2,1)S(1)} %bitcast.203, pred[256]{0:T(512)(128)(4,1)S(1)} %compare_and_fusion.2, f32[1,256,350]{1,2,0:T(8,128)S(1)} %get-tuple-element.22, ...), kind=kOutput, calls=%fused_computation.11 | convolution fusion | flops 3306339328 | bytes 9736448 | tf_op jit(solution)/shard_map/sba,sbtf->satf/dot_general | solution.py:74
  190.8 0.0 all-reduce.7.cloned.1.call-update
  190.9 0.7 copy-done.11
  191.5 0.1 copy.74
  191.6 0.1 copy-done.7
  191.8 0.2 fusion.45
  192.0 0.2 convolution_add_fusion.4
  192.2 0.2 convolution_add_fusion.3
  192.5 0.2 convolution_add_fusion.5
  192.7 0.2 convolution_add_fusion.2
  193.0 0.2 convolution_add_fusion.1
  193.2 0.2 fusion.28
  193.5 0.0 copy-done.9
  193.5 0.1 reduce_sum.19
  193.6 160.5 %all-reduce.7.cloned.1.call-done = f32[2,350,1536]{2,1,0:T(8,128)} async-done(((f32[2,350,1536]{2,1,0:T(8,128)}), f32[2,350,1536]{2,1,0:T(8,128)}) %all-reduce.7.cloned.1.call-update) | async-done | bytes 4300816 | tf_op jit(solution)/shard_map/psum | solution.py:77
  354.1 0.0 copy-done
  354.1 9.4 %fusion.29 = f32[2,1536,350]{1,2,0:T(8,128)S(1)} fusion(f32[2,350,1536]{2,1,0:T(8,128)} %all-reduce.7.cloned.1.call-done, f32[2,350,350]{2,0,1:T(2,128)S(1)} %copy-done), kind=kOutput, calls=%fused_computation.56 | convolution fusion | flops 4515840000 | bytes 9581600 | tf_op jit(solution)/shard_map/sab,sbtf->satf/dot_general | solution.py:42
  363.5 0.0 copy-start.2
  363.5 1.8 slice_bitcast_fusion.1
  365.4 0.8 copy-done.2
  366.2 4.7 %gather_fusion.2 = f32[256,1536]{1,0:T(8,128)} fusion(f32[350,1536]{1,0:T(8,128)} %get-tuple-element.19, s32[1024]{0:T(1024)S(1)} %pad_clamp_fusion), kind=kCustom, calls=%fused_computation.1.clone | custom fusion | bytes 3146752 | tf_op jit(solution)/shard_map/jit(_take)/gather | solution.py:84
  370.9 4.7 %gather_fusion.1 = f32[256,1536]{1,0:T(8,128)} fusion(f32[350,1536]{1,0:T(8,128)} %get-tuple-element.19, s32[1024]{0:T(1024)S(1)} %pad_clamp_fusion.1), kind=kCustom, calls=%fused_computation.clone | custom fusion | bytes 3146752 | tf_op jit(solution)/shard_map/jit(_take)/gather | solution.py:83
  375.7 2.3 gather_fusion.3
  378.0 2.3 gather_fusion.4
  380.3 0.0 copy-done.5
  380.3 9.3 %fusion.31 = (bf16[1,256,1,1536]{3,1,2,0:T(8,128)(2,1)S(1)}, bf16[1,256,1,1536]{3,1,2,0:T(8,128)(2,1)S(1)}) fusion(f32[256,1536]{1,0:T(8,128)} %gather_fusion.4, pred[256]{0:T(512)(128)(4,1)S(1)} %get-tuple-element.25, f32[256,1536]{1,0:T(8,128)} %gather_fusion.3, pred[256]{0:T(512)(128)(4,1)S(1)} %get-tuple-element.26, ...), kind=kLoop, calls=%fused_computation.58 | loop fusion | flops 5505024 | bytes 9437696 | tf_op jit(solution)/shard_map/stack | solution.py:92
  389.7 0.1 pad_maximum_fusion
  389.8 2.8 copy.58
  392.6 7.5 %all-to-all-start = ((bf16[2,256,1,1536]{3,0,2,1:T(2,128)(2,1)}), bf16[2,256,1,1536]{3,0,2,1:T(2,128)(2,1)S(1)}, u32[]{:S(2)}, u32[]{:S(2)}) async-start(bf16[2,256,1,1536]{3,0,2,1:T(2,128)(2,1)} %copy.58), calls=%async_computation | async-start | bytes 3145728 | tf_op jit(solution)/shard_map/all_to_all | solution.py:96
  400.1 0.1 broadcast_in_dim.34.clone
  400.3 1.4 broadcast_multiply_fusion
  401.7 8.7 %copy.63 = f32[2,350,1,1536]{3,2,1,0:T(1,128)} copy(f32[2,350,1,1536]{3,1,0,2:T(8,128)} %bitcast.199) | data formatting | bytes 8601600
  410.5 10.2 %all-to-all-done = bf16[2,256,1,1536]{3,0,2,1:T(2,128)(2,1)S(1)} async-done(((bf16[2,256,1,1536]{3,0,2,1:T(2,128)(2,1)}), bf16[2,256,1,1536]{3,0,2,1:T(2,128)(2,1)S(1)}, u32[]{:S(2)}, u32[]{:S(2)}) %all-to-all-start) | async-done | bytes 1572896 | tf_op jit(solution)/shard_map/all_to_all | solution.py:96
  420.7 0.0 copy-done.8
  420.7 1.1 fusion.18
  421.8 1.1 fusion.60
  422.9 1.2 fusion.58
  424.0 1.2 fusion.56
  425.3 2.9 fusion.53
  428.2 2.9 fusion.51
  431.1 2.9 fusion.49
  434.0 0.0 copy-done.3
  434.0 11.8 %fusion.1 = f32[2,32,8,1536]{3,2,1,0:T(8,128)} fusion(f32[2,32,8,12,128]{4,2,3,1,0:T(8,128)} %fusion.49, f32[2,32,8,12,128]{4,2,3,1,0:T(8,128)} %fusion.51, f32[2,32,8,12,128]{4,2,3,1,0:T(8,128)} %fusion.53, f32[2,32,8,12,128]{4,2,3,1,0:T(8,128)S(1)} %fusion.18, f32[2,32,8,12,128]{4,2,3,1,0:T(8,128)S(1)} %fusion.56, f32[2,32,8,12,128]{4,2,3,1,0:T(8,128)S(1)} %fusion.60, ...), kind=kOutput, calls=%fused_computation.8 | convolution fusion | flops 84148224 | bytes 28705024 | tf_op jit(solution)/shard_map/tu,kbuf->kbtf/dot_general | solution.py:32
  445.7 0.0 copy-done.1
  (20 shorter events, 0.1 us)
Async XLA Ops:
  7.2 347.0 %copy-start = (f32[2,350,350]{2,0,1:T(2,128)S(1)}, f32[2,350,350]{2,0,1:T(2,128)}, u32[]{:S(2)}) copy-start(f32[2,350,350]{2,0,1:T(2,128)} %param.15) | copy-start | bytes 2940004
  7.2 161.8 %all-reduce.5.cloned.1.call-start = ((), (), s32[]{:S(2)}) async-start(), calls=%async_computation.1 | async-start | bytes 5505024 | tf_op jit(solution)/shard_map/psum | solution.py:69
  10.7 0.7 copy-start.10
  10.7 65.6 %copy-start.12 = (s32[256,2]{0,1:T(2,128)S(1)}, s32[256,2]{0,1:T(2,128)}, u32[]{:S(2)}) copy-start(s32[256,2]{0,1:T(2,128)} %param.13) | copy-start | bytes 6148
  10.8 343.4 %all-reduce.7.cloned.1.call-start = ((), (), s32[]{:S(2)}) async-start(), calls=%async_computation.2 | async-start | bytes 8650752 | tf_op jit(solution)/shard_map/psum | solution.py:77
  174.7 7.3 %copy-start.4 = (bf16[256,1,1536]{2,0,1:T(8,128)(2,1)S(1)}, bf16[256,1,1536]{2,0,1:T(8,128)(2,1)}, u32[]{:S(2)}) copy-start(bf16[256,1,1536]{2,0,1:T(8,128)(2,1)} %param.11) | copy-start | bytes 2359300
  174.7 7.3 %copy-start.6 = (bf16[256,1,1536]{2,0,1:T(8,128)(2,1)S(1)}, bf16[256,1,1536]{2,0,1:T(8,128)(2,1)}, u32[]{:S(2)}) copy-start(bf16[256,1,1536]{2,0,1:T(8,128)(2,1)} %param.10) | copy-start | bytes 2359300
  190.8 0.7 copy-start.11
  190.8 1.0 copy-start.7
  191.8 1.7 copy-start.9
  363.5 2.7 copy-start.2
  378.0 2.3 copy-start.5
  392.6 28.1 %all-to-all-start = ((bf16[2,256,1,1536]{3,0,2,1:T(2,128)(2,1)}), bf16[2,256,1,1536]{3,0,2,1:T(2,128)(2,1)S(1)}, u32[]{:S(2)}, u32[]{:S(2)}) async-start(bf16[2,256,1,1536]{3,0,2,1:T(2,128)(2,1)} %copy.58), calls=%async_computation | async-start | bytes 3145728 | tf_op jit(solution)/shard_map/all_to_all | solution.py:96
  401.7 19.0 %copy-start.8 = (bf16[7,128,128]{2,1,0:T(8,128)(2,1)S(1)}, bf16[7,128,128]{2,1,0:T(8,128)(2,1)}, u32[]{:S(2)}) copy-start(bf16[7,128,128]{2,1,0:T(8,128)(2,1)} %param.17) | copy-start | bytes 688132
  431.0 2.9 copy-start.3
  434.0 11.8 %copy-start.1 = (f32[2,350,350]{2,0,1:T(2,128)S(1)}, f32[2,350,350]{2,0,1:T(2,128)}, u32[]{:S(2)}) copy-start(f32[2,350,350]{2,0,1:T(2,128)} %param.15) | copy-start | bytes 2940004
Sparse Core Ops, SparseCore 0:
  12.1 156.7 all-reduce.4
  191.0 163.1 all-reduce.6
where the time goes:
time: 461 us; the launch traced here: 453 us
  waiting for transfers between devices  263 us (57%)
  blocking collectives  64.8 us (14%)
  matrix products  48.4 us (10%)
  local copies, waits for them, and re-layouts  41 us (9%)
  between operations  14.5 us (3%)
  other arithmetic  13.4 us (3%)
  starting transfers between devices  7.6 us (2%)
    psum x1, waiting for transfers between devices, on_device(): normal_right_side = lax.psum(rhs_part, 'bl')  161 us
    psum x1, waiting for transfers between devices, on_device(): group_sums, group_counts = lax.psum((group_part, count_part), 'bl')  92.5 us
    psum x1, blocking collectives, on_device(): group_sums, group_counts = lax.psum((group_part, count_part), 'bl')  64.8 us
    dot_general x14, matrix products, mix_channels(): jnp.einsum('...kj,ij->...ki', window, channel_kernel[offset], preferred_e...  14.9 us
    dot_general x1, matrix products, fill_block(): jnp.einsum('tu,kbuf->kbtf', integration_kernel, mixed, precision=lax.Prec...  11.8 us
    unnamed x28, local copies, waits for them, and re-layouts  11.1 us
    all_to_all x1, waiting for transfers between devices, on_device(): lax.all_to_all(calibrated, 'ta', split_axis=1, concat_axis=2, tiled=True)  10.2 us
    another operation x2, other arithmetic, on_device(): jnp.stack([magnitude * jnp.cos(calibrated_phase), magnitude * jnp.sin(cal...  9.48 us
  transfers between devices with their start and end apart: 3, of which 3 were waited for; matrix products, arithmetic and copies ran while one was open for 3% of the time, Pallas kernels for 0%

commit v1 on v0

--- a/solution.py
+++ b/solution.py
@@ -74,7 +74,11 @@
     rhs_part = jnp.einsum(
         "sba,sbtf->satf", signed_float, fit_residual, precision=lax.Precision.HIGHEST
     )
-    normal_right_side = lax.psum(rhs_part, "bl")
+    normal_right_side = rhs_part
+    for hop in (1, 2, 4, 8, 16):
+        normal_right_side = normal_right_side + lax.ppermute(
+            normal_right_side, "bl", [(dev, dev ^ hop) for dev in range(32)]
+        )
     antenna_gains = solve_columns(inverse, normal_right_side)
     amplitude_gain = antenna_gains[0]
     phase_gain_term = antenna_gains[1]

time: 461 us -> 976 us (2.12)
  waiting for transfers between devices: 263 us -> 750 us
  local copies, waits for them, and re-layouts: 41 us -> 58.4 us
    ppermute x0 -> x5, waiting for transfers between devices: none -> 646 us  [on_device(): lax.ppermute(normal_right_side, 'bl', [(dev, dev ^ hop) for dev in range(...]
    psum x1 -> x0, waiting for transfers between devices: 161 us -> none  [on_device(): normal_right_side = lax.psum(rhs_part, 'bl')]
    add x0 -> x4, local copies, waits for them, and re-layouts: none -> 15.3 us  [on_device(): normal_right_side + lax.ppermute(normal_right_side, 'bl', [(dev, dev ^ ho...]
  transfers between devices with their start and end apart: 3 -> 7, of which waited for: 3 -> 7; matrix products, arithmetic and copies ran while one was open for 3% -> 1% of each run, Pallas kernels for 0% -> 0%
where the time goes in v1:
time: 976 us; the launch traced here: 966 us
  waiting for transfers between devices  750 us (77%)
  blocking collectives  64.7 us (7%)
  local copies, waits for them, and re-layouts  58.4 us (6%)
  matrix products  46.5 us (5%)
  other arithmetic  17.7 us (2%)
  between operations  14.8 us (2%)
  starting transfers between devices  14.5 us (1%)
    ppermute x5, waiting for transfers between devices, on_device(): lax.ppermute(normal_right_side, 'bl', [(dev, dev ^ hop) for dev in range(...  646 us
    psum x1, waiting for transfers between devices, on_device(): group_sums, group_counts = lax.psum((group_part, count_part), 'bl')  93.2 us
    psum x1, blocking collectives, on_device(): group_sums, group_counts = lax.psum((group_part, count_part), 'bl')  64.7 us
  transfers between devices with their start and end apart: 7, of which 7 were waited for; matrix products, arithmetic and copies ran while one was open for 1% of the time, Pallas kernels for 0%

profile of v1, /device:TPU:1, one launch (start us, length us, event | category | flops | bytes accessed | tf_op | source)
XLA Modules:
  0.0 966.2 jit_solution(12369519201613334938)
XLA Ops:
  7.2 0.0 copy-start
  7.2 0.0 all-reduce.4.cloned.1.call-start
  7.2 3.5 convolution_bitcast_fusion.1
  10.8 0.0 all-reduce.4.cloned.1.call-update
  10.8 0.1 convert_reduce_fusion
  10.9 64.7 %psum.15 = f32[224]{0:T(256)S(1)} all-reduce(f32[224]{0:T(256)S(1)} %convert_reduce_fusion), channel_id=1, replica_groups=mesh['bl'=32,'ta'=8] {'bl'}, use_global_device_ids=true, to_apply=%region_2.0 | all-reduce | flops 224 | bytes 1792 | tf_op jit(solution)/shard_map/psum | solution.py:69
  75.6 0.1 convert_add_fusion
  75.7 93.2 %all-reduce.4.cloned.1.call-done = f32[2,224,1,1536]{3,1,0,2:T(8,128)} async-done(((f32[2,224,1,1536]{3,1,0,2:T(8,128)}), f32[2,224,1,1536]{3,1,0,2:T(8,128)}) %all-reduce.4.cloned.1.call-update) | async-done | bytes 2752528 | tf_op jit(solution)/shard_map/psum | solution.py:69
  168.9 2.1 divide_bitcast_fusion
  171.0 3.7 copy.75
  174.6 7.3 gather_fusion
  181.9 6.4 convolution_bitcast_fusion
  188.4 3.5 copy.77
  191.9 0.6 collective-permute-start
  192.5 89.6 %collective-permute-done = f32[2,350,1,1536]{3,0,2,1:T(2,128)S(1)} collective-permute-done((f32[2,350,1,1536]{3,0,2,1:T(2,128)S(1)}, f32[2,350,1,1536]{3,0,2,1:T(2,128)S(1)}, u32[]{:S(2)}, u32[]{:S(2)}) %collective-permute-start) | collective-permute-done | bytes 4300832 | tf_op jit(solution)/shard_map/ppermute | solution.py:79
  282.1 1.1 copy_add_fusion.5
  283.2 3.3 copy.79
  286.5 1.1 collective-permute-start.1
  287.6 186.7 %collective-permute-done.1 = f32[2,350,1,1536]{3,0,2,1:T(2,128)S(1)} collective-permute-done((f32[2,350,1,1536]{3,0,2,1:T(2,128)S(1)}, f32[2,350,1,1536]{3,0,2,1:T(2,128)S(1)}, u32[]{:S(2)}, u32[]{:S(2)}) %collective-permute-start.1) | collective-permute-done | bytes 4300832 | tf_op jit(solution)/shard_map/ppermute | solution.py:79
  474.3 1.1 copy_add_fusion.4
  475.4 3.3 copy.81
  478.8 0.7 collective-permute-start.2
  479.4 187.4 %collective-permute-done.2 = f32[2,350,1,1536]{3,0,2,1:T(2,128)S(1)} collective-permute-done((f32[2,350,1,1536]{3,0,2,1:T(2,128)S(1)}, f32[2,350,1,1536]{3,0,2,1:T(2,128)S(1)}, u32[]{:S(2)}, u32[]{:S(2)}) %collective-permute-start.2) | collective-permute-done | bytes 4300832 | tf_op jit(solution)/shard_map/ppermute | solution.py:79
  666.8 1.1 copy_add_fusion.3
  667.9 3.3 copy.83
  671.2 0.3 collective-permute-start.3
  671.5 92.8 %collective-permute-done.3 = f32[2,350,1,1536]{3,0,2,1:T(2,128)S(1)} collective-permute-done((f32[2,350,1,1536]{3,0,2,1:T(2,128)S(1)}, f32[2,350,1,1536]{3,0,2,1:T(2,128)S(1)}, u32[]{:S(2)}, u32[]{:S(2)}) %collective-permute-start.3) | collective-permute-done | bytes 4300832 | tf_op jit(solution)/shard_map/ppermute | solution.py:79
  764.2 1.1 copy_add_fusion.2
  765.3 0.0 copy-start.12
  765.4 5.4 copy.85
  770.7 4.5 collective-permute-start.4
  775.3 0.1 copy.105
  775.4 0.2 fusion.45
  775.6 0.2 convolution_add_fusion.4
  775.8 0.2 convolution_add_fusion.3
  776.1 0.2 convolution_add_fusion.5
  776.3 0.2 convolution_add_fusion.2
  776.5 0.2 convolution_add_fusion.1
  776.8 0.2 fusion.29
  777.1 0.1 reduce_sum.19
  777.2 89.8 %collective-permute-done.4 = f32[2,350,1,1536]{3,0,2,1:T(2,128)} collective-permute-done((f32[2,350,1,1536]{3,0,2,1:T(2,128)}, f32[2,350,1,1536]{3,0,2,1:T(2,128)}, u32[]{:S(2)}, u32[]{:S(2)}) %collective-permute-start.4) | collective-permute-done | bytes 4300832 | tf_op jit(solution)/shard_map/ppermute | solution.py:79
  867.0 9.8 %fusion = f32[2,1536,350]{1,2,0:T(8,128)S(1)} fusion(f32[2,350,1,1536]{3,1,0,2:T(8,128)} %copy-done.3, f32[2,350,1,1536]{3,0,2,1:T(2,128)} %collective-permute-done.4, f32[2,350,350]{2,0,1:T(2,128)S(1)} %copy-done), kind=kOutput, calls=%fused_computation.5 | convolution fusion | flops 4516915200 | bytes 13882400 | tf_op jit(solution)/shard_map/sab,sbtf->satf/dot_general | solution.py:42
  876.9 1.8 slice_bitcast_fusion.1
  878.7 0.8 copy-done.2
  879.6 4.7 gather_fusion.2
  884.3 4.7 gather_fusion.1
  889.0 2.3 gather_fusion.3
  891.3 2.3 gather_fusion.4
  893.7 9.3 fusion.31
  903.0 0.1 pad_maximum_fusion
  903.2 2.8 copy.89
  905.9 7.3 all-to-all-start
  913.2 0.1 broadcast_in_dim.34.clone
  913.4 1.4 broadcast_multiply_fusion
  914.8 8.7 copy.94
  923.6 10.2 %all-to-all-done = bf16[2,256,1,1536]{3,0,2,1:T(2,128)(2,1)S(1)} async-done(((bf16[2,256,1,1536]{3,0,2,1:T(2,128)(2,1)}), bf16[2,256,1,1536]{3,0,2,1:T(2,128)(2,1)S(1)}, u32[]{:S(2)}, u32[]{:S(2)}) %all-to-all-start) | async-done | bytes 1572896 | tf_op jit(solution)/shard_map/all_to_all | solution.py:100
  933.8 1.1 fusion.19
  934.8 1.1 fusion.60
  935.9 1.2 fusion.58
  937.1 1.2 fusion.56
  938.3 2.9 fusion.53
  941.3 2.9 fusion.51
  944.1 3.0 fusion.49
  947.1 11.8 %fusion.3 = f32[2,32,8,1536]{3,2,1,0:T(8,128)} fusion(f32[2,32,8,12,128]{4,2,3,1,0:T(8,128)} %fusion.49, f32[2,32,8,12,128]{4,2,3,1,0:T(8,128)} %fusion.51, f32[2,32,8,12,128]{4,2,3,1,0:T(8,128)} %fusion.53, f32[2,32,8,12,128]{4,2,3,1,0:T(8,128)S(1)} %fusion.19, f32[2,32,8,12,128]{4,2,3,1,0:T(8,128)S(1)} %fusion.56, f32[2,32,8,12,128]{4,2,3,1,0:T(8,128)S(1)} %fusion.60, ...), kind=kOutput, calls=%fused_computation.16 | convolution fusion | flops 84148224 | bytes 28705024 | tf_op jit(solution)/shard_map/tu,kbuf->kbtf/dot_general | solution.py:32
  (38 shorter events, 0.2 us)
Async XLA Ops:
  7.2 859.9 %copy-start = (f32[2,350,350]{2,0,1:T(2,128)S(1)}, f32[2,350,350]{2,0,1:T(2,128)}, u32[]{:S(2)}) copy-start(f32[2,350,350]{2,0,1:T(2,128)} %param.15) | copy-start | bytes 2940004
  7.2 161.7 %all-reduce.4.cloned.1.call-start = ((), (), s32[]{:S(2)}) async-start(), calls=%async_computation.1 | async-start | bytes 5505024 | tf_op jit(solution)/shard_map/psum | solution.py:69
  7.2 3.6 copy-start.11
  7.2 68.4 %copy-start.13 = (s32[256,2]{0,1:T(2,128)S(1)}, s32[256,2]{0,1:T(2,128)}, u32[]{:S(2)}) copy-start(s32[256,2]{0,1:T(2,128)} %param.13) | copy-start | bytes 6148
  174.6 7.3 copy-start.5
  174.6 7.3 copy-start.7
  191.9 90.2 %collective-permute-start = (f32[2,350,1,1536]{3,0,2,1:T(2,128)S(1)}, f32[2,350,1,1536]{3,0,2,1:T(2,128)S(1)}, u32[]{:S(2)}, u32[]{:S(2)}) collective-permute-start(f32[2,350,1,1536]{3,0,2,1:T(2,128)S(1)} %copy.77), channel_id=1, source_target_pairs={{0,8},{8,0},{16,24},{24,16},{32,40},{40,32},{48,56},{56,48},{64,72... | collective-permute-start | bytes 12902408 | tf_op jit(solution)/shard_map/ppermute | solution.py:79
  286.5 187.8 %collective-permute-start.1 = (f32[2,350,1,1536]{3,0,2,1:T(2,128)S(1)}, f32[2,350,1,1536]{3,0,2,1:T(2,128)S(1)}, u32[]{:S(2)}, u32[]{:S(2)}) collective-permute-start(f32[2,350,1,1536]{3,0,2,1:T(2,128)S(1)} %copy.79), channel_id=1, source_target_pairs={{0,16},{8,24},{16,0},{24,8},{32,48},{40,56},{48,32},{56,40},{64,80... | collective-permute-start | bytes 12902408 | tf_op jit(solution)/shard_map/ppermute | solution.py:79
  478.8 188.0 %collective-permute-start.2 = (f32[2,350,1,1536]{3,0,2,1:T(2,128)S(1)}, f32[2,350,1,1536]{3,0,2,1:T(2,128)S(1)}, u32[]{:S(2)}, u32[]{:S(2)}) collective-permute-start(f32[2,350,1,1536]{3,0,2,1:T(2,128)S(1)} %copy.81), channel_id=1, source_target_pairs={{0,32},{8,40},{16,48},{24,56},{32,0},{40,8},{48,16},{56,24},{64,96... | collective-permute-start | bytes 12902408 | tf_op jit(solution)/shard_map/ppermute | solution.py:79
  671.2 93.0 %collective-permute-start.3 = (f32[2,350,1,1536]{3,0,2,1:T(2,128)S(1)}, f32[2,350,1,1536]{3,0,2,1:T(2,128)S(1)}, u32[]{:S(2)}, u32[]{:S(2)}) collective-permute-start(f32[2,350,1,1536]{3,0,2,1:T(2,128)S(1)} %copy.83), channel_id=1, source_target_pairs={{0,64},{8,72},{16,80},{24,88},{32,96},{40,104},{48,112},{56,120},{... | collective-permute-start | bytes 12902408 | tf_op jit(solution)/shard_map/ppermute | solution.py:79
  765.3 5.4 copy-start.3
  765.3 9.9 %copy-start.12 = (s32[32,12]{0,1:T(8,128)S(1)}, s32[32,12]{0,1:T(8,128)}, u32[]{:S(2)}) copy-start(s32[32,12]{0,1:T(8,128)} %param.14) | copy-start | bytes 4612
  765.4 10.0 %copy-start.8 = (bf16[7,128,128]{2,1,0:T(8,128)(2,1)S(1)}, bf16[7,128,128]{2,1,0:T(8,128)(2,1)}, u32[]{:S(2)}) copy-start(bf16[7,128,128]{2,1,0:T(8,128)(2,1)} %param.17) | copy-start | bytes 688132
  770.7 6.3 copy-start.10
  770.7 96.3 %collective-permute-start.4 = (f32[2,350,1,1536]{3,0,2,1:T(2,128)}, f32[2,350,1,1536]{3,0,2,1:T(2,128)}, u32[]{:S(2)}, u32[]{:S(2)}) collective-permute-start(f32[2,350,1,1536]{3,0,2,1:T(2,128)} %copy.85), channel_id=1, source_target_pairs={{0,128},{8,136},{16,144},{24,152},{32,160},{40,168},{48,176},{56,1... | collective-permute-start | bytes 12902408 | tf_op jit(solution)/shard_map/ppermute | solution.py:79
  876.9 2.7 copy-start.2
  891.3 2.3 copy-start.6
  905.9 27.8 %all-to-all-start = ((bf16[2,256,1,1536]{3,0,2,1:T(2,128)(2,1)}), bf16[2,256,1,1536]{3,0,2,1:T(2,128)(2,1)S(1)}, u32[]{:S(2)}, u32[]{:S(2)}) async-start(bf16[2,256,1,1536]{3,0,2,1:T(2,128)(2,1)} %copy.89), calls=%async_computation | async-start | bytes 3145728 | tf_op jit(solution)/shard_map/all_to_all | solution.py:100
  914.8 18.9 %copy-start.9 = (bf16[7,128,128]{2,1,0:T(8,128)(2,1)S(1)}, bf16[7,128,128]{2,1,0:T(8,128)(2,1)}, u32[]{:S(2)}) copy-start(bf16[7,128,128]{2,1,0:T(8,128)(2,1)} %param.17) | copy-start | bytes 688132
  944.1 3.0 copy-start.4
  947.1 11.8 %copy-start.1 = (f32[2,350,350]{2,0,1:T(2,128)S(1)}, f32[2,350,350]{2,0,1:T(2,128)}, u32[]{:S(2)}) copy-start(f32[2,350,350]{2,0,1:T(2,128)} %param.15) | copy-start | bytes 2940004
Sparse Core Ops, SparseCore 0:
  12.1 156.7 all-reduce.3
